TPU v7x, 512 devices: a whole 4x8x8 slice. The times are simulated.
512 devices in a mesh: ctx: 32 (over z_lo, x, core), tp: 16 (over z_hi, y).
Axes of the slice: x: 4, y: 8, z: 8 (z_hi: 2, z_lo: 4; z = z_hi * 4 + z_lo), core: 2. Of those that a mesh axis runs over, the one named last changes fastest.
Arguments:
- queries: bfloat16 [8192, 8192], P('ctx', 'tp'), may hold values from -100 to 100
- key_rows: bfloat16 [8192, 1024], P('ctx'), may hold values from -5 to 5
- value_rows: bfloat16 [8192, 1024], P('ctx'), may hold values from -6 to 6
- documents: int32 [8192], P('ctx'), may hold values from 0 to 3, never falling along the last dimension, each value on 1 to 6144 neighbouring positions
- out_weight: bfloat16 [8192, 8192], P('tp', 'ctx'), may hold values from -0.75 to 0.75
Outputs:
- attention_out: bfloat16 [8192, 8192], P(('ctx', 'tp'))
Inputs may be any that keep to these rules, and one draw needn't show every extreme that they name: `documents`: document numbers never fall along the window; each document holds 1 to 6144 tokens and one holds exactly 6144.
All inputs are finite; a program needn't handle non-finite values.
Results may differ from a plain program's by a relative error of at most 0.015.
Values may be sent and summed in bfloat16 or wider, within the bound.
No kernel may reach another device: no remote copies, remote signals or barrier semaphores. Data moves between devices by JAX's collectives and lax.ppermute only.
A program may use at most 128 MiB of HBM per device.

v0:
```python
import math
import jax
import jax.numpy as jnp
from jax import lax
from jax.sharding import PartitionSpec as P

HEADS = 64
KV_HEADS = 8
HD = 128


def absorb_group(state, query_block, query_pos, query_docs, piece, start):
    piece_keys, piece_values, piece_docs = piece
    length = piece_keys.shape[0]
    kv_here = query_block.shape[1]
    scale = 1.0 / math.sqrt(HD)

    def update(inner):
        old_max, old_sum, old_acc = inner
        key_block = piece_keys.reshape(length, kv_here, HD)
        value_block = piece_values.reshape(length, kv_here, HD)
        scores = (
            jnp.einsum("tghd,ngd->ghtn", query_block, key_block, preferred_element_type=jnp.float32)
            * scale
        )
        key_pos = jnp.arange(length, dtype=jnp.int32)
        allowed = (key_pos[None, :] <= query_pos[:, None]) & (
            piece_docs[None, :] == query_docs[:, None]
        )
        new_max = jnp.maximum(old_max, jnp.max(jnp.where(allowed, scores, -1e30), axis=3))
        weights = jnp.where(allowed, jnp.exp(scores - new_max[..., None]), 0.0)
        new_sum = jnp.sum(weights, axis=3)
        weighted = jnp.einsum(
            "ghtn,ngd->tghd",
            weights.astype(jnp.bfloat16),
            value_block,
            preferred_element_type=jnp.float32,
        )
        return (new_max, new_sum, weighted)

    return lax.cond(start <= query_pos[-1], update, lambda inner: inner, state)


def empty_state(rows, kv_here, per_kv):
    return (
        jnp.full((kv_here, per_kv, rows), -1e30, jnp.float32),
        jnp.zeros((kv_here, per_kv, rows), jnp.float32),
        jnp.zeros((rows, kv_here, per_kv, HD), jnp.float32),
    )


def finish(state):
    run_max, run_sum, run_acc = state
    rows = run_acc.shape[0]
    attended = (run_acc / jnp.transpose(run_sum, (2, 0, 1))[..., None]).astype(jnp.bfloat16)
    return attended.reshape(rows, run_acc.shape[1] * run_acc.shape[2] * HD)


def on_device(queries, key_rows, value_rows, documents, out_weight):
    tokens_here = queries.shape[0]
    heads_here = queries.shape[1] // HD
    group_size = HEADS // KV_HEADS
    kv_here = max(1, heads_here // group_size)
    per_kv = heads_here // kv_here
    kv_first = lax.axis_index("tp") * heads_here // group_size
    own_keys = lax.dynamic_slice_in_dim(key_rows, kv_first * HD, kv_here * HD, 1)
    own_values = lax.dynamic_slice_in_dim(value_rows, kv_first * HD, kv_here * HD, 1)
    query_blocks = queries.reshape(tokens_here, kv_here, per_kv, HD)
    first_row = lax.axis_index("ctx") * tokens_here
    groups = [(query_blocks, first_row + jnp.arange(tokens_here, dtype=jnp.int32), documents)]
    initial = tuple((empty_state(group[0].shape[0], kv_here, per_kv) for group in groups))
    piece = (
        lax.all_gather(own_keys, "ctx", axis=0, tiled=True),
        lax.all_gather(own_values, "ctx", axis=0, tiled=True),
        lax.all_gather(documents, "ctx", axis=0, tiled=True),
    )
    start = jnp.int32(0)
    states = tuple(
        (
            absorb_group(
                initial[index], groups[index][0], groups[index][1], groups[index][2], piece, start
            )
            for index in range(len(groups))
        )
    )
    attended = finish(states[0])
    terms = jnp.dot(
        attended,
        lax.all_gather(out_weight, "ctx", axis=1, tiled=True),
        preferred_element_type=jnp.float32,
    )
    summed = lax.psum_scatter(terms.astype(jnp.bfloat16), "tp", scatter_dimension=0, tiled=True)
    return summed


def solution(mesh):
    in_specs = (P("ctx", "tp"), P("ctx", None), P("ctx", None), P("ctx"), P("tp", "ctx"))
    out_specs = P(("ctx", "tp"), None)
    return jax.shard_map(
        on_device, mesh=mesh, in_specs=in_specs, out_specs=out_specs, check_vma=False
    )
```

profile of v0, /device:TPU:2, one launch (start us, length us, event | category | flops | bytes accessed | tf_op | source)
XLA Modules:
  0.0 487.1 jit_solution(4593538375489686162)
XLA Ops:
  6.5 0.0 copy-start
  6.5 0.0 all-gather.5.cloned.1.call-start
  6.5 1.0 copy-done
  7.6 0.6 constant_dynamic-slice_fusion.1
  8.2 0.0 all-gather.5.cloned.1.call-update
  8.2 0.0 all-gather.7.cloned.1.call-start
  8.3 1.5 constant_dynamic-slice_fusion
  9.8 0.0 all-gather.7.cloned.1.call-update
  9.8 0.0 all-gather.9.cloned.1.call-start
  9.8 0.7 all-gather.9.cloned.1.call-update
  10.5 0.0 reduce-scatter.2.cloned.1.call-start
  10.6 0.6 slice.3
  11.9 43.7 %all-gather = s32[32,1,256]{2,1,0:T(1,128)S(1)} all-gather(s32[1,1,256]{2,1,0:T(1,128)} %bitcast.64), channel_id=1, replica_groups=mesh['ctx'=32,'tp'=16] {'ctx'}, dimensions={0}, use_global_device_ids=true | all-gather | bytes 33792 | tf_op jit(solution)/shard_map/all_gather | solution.py:75
  55.6 21.2 %all-gather.5.cloned.1.call-done = bf16[8192,128]{1,0:T(8,128)(2,1)} async-done(((bf16[256,128]{1,0:T(8,128)(2,1)}), bf16[8192,128]{1,0:T(8,128)(2,1)}) %all-gather.5.cloned.1.call-update) | async-done | bytes 2097168 | tf_op jit(solution)/shard_map/all_gather | solution.py:73
  76.7 63.6 %all-gather.7.cloned.1.call-done = bf16[8192,128]{1,0:T(8,128)(2,1)} async-done(((bf16[256,128]{1,0:T(8,128)(2,1)}), bf16[8192,128]{1,0:T(8,128)(2,1)}) %all-gather.7.cloned.1.call-update) | async-done | bytes 2097168 | tf_op jit(solution)/shard_map/all_gather | solution.py:74
  140.4 49.9 %conditional.1 = (f32[1,4,256]{2,1,0:T(4,128)S(1)}, f32[256,1,4,128]{0,3,2,1:T(8,128)S(1)}) conditional(s32[]{:T(128)} %bitcast.10, () %tuple.13, (s32[256]{0:T(256)S(1)}, s32[8192]{0:T(1024)S(1)}, s32[256]{0:T(256)}, bf16[256,512]{1,0:T(8,128)(2,1)}, bf16[8192,128]{1,0:T(8,128)(2,1)}, /*index=5*/bf16[8192,128]{1,0:T(8,128)(2,1)}) %tuple.28), branch_computations={%region_0.1_spmd, %region_1.4_spmd} | conditional | flops 4393532416 | bytes 115140624 | solution.py:41
  140.4 4.4 fusion.9
  144.8 14.9 %fusion = (f32[4,256]{1,0:T(4,128)S(1)}, f32[8192,256,4]{1,0,2:T(8,128)}) fusion(pred[256,8192]{0,1:T(8,128)(4,1)S(1)} %fusion.9, bf16[8192,128]{1,0:T(8,128)(2,1)} %get-tuple-element.21, bf16[256,512]{1,0:T(8,128)(2,1)} %get-tuple-element.29), kind=kOutput, calls=%fused_computation.2 | convolution fusion | flops 2172648448 | bytes 38014976 | tf_op jit(solution)/shard_map/cond/branch_1_fun/tghd,ngd->ghtn/dot_general | solution.py:23
  159.8 14.8 %fusion.4 = f32[4,256]{1,0:T(4,128)S(1)} fusion(f32[8192,256,4]{1,0,2:T(8,128)} %get-tuple-element.32, f32[4,256]{1,0:T(4,128)S(1)} %broadcast_maximum_fusion, pred[256,8192]{0,1:T(8,128)(4,1)S(1)} %fusion.9), kind=kLoop, calls=%fused_computation.6 | loop fusion | flops 33553408 | bytes 35659776 | tf_op jit(solution)/shard_map/cond/branch_1_fun/reduce_sum | solution.py:32
  174.5 15.5 %fusion.13 = f32[256,1,4,128]{3,0,2,1:T(8,128)S(1)} fusion(bf16[8192,128]{1,0:T(8,128)(2,1)} %get-tuple-element.23, f32[8192,256,4]{1,0,2:T(8,128)} %get-tuple-element.32, f32[4,256]{1,0:T(4,128)S(1)} %broadcast_maximum_fusion, pred[256,8192]{0,1:T(8,128)(4,1)S(1)} %fusion.9), kind=kOutput, calls=%fused_computation.15 | convolution fusion | flops 2181038080 | bytes 38277120 | tf_op jit(solution)/shard_map/cond/branch_1_fun/ghtn,ngd->tghd/dot_general | solution.py:33
  190.1 0.2 copy.17
  190.3 40.4 %all-gather.9.cloned.1.call-done = bf16[512,8192]{1,0:T(8,128)(2,1)} async-done(((bf16[512,256]{1,0:T(8,128)(2,1)}), bf16[512,8192]{1,0:T(8,128)(2,1)}) %all-gather.9.cloned.1.call-update) | async-done | bytes 8388624 | tf_op jit(solution)/shard_map/all_gather | solution.py:89
  230.7 7.7 %convolution_convert_fusion = bf16[256,8192]{1,0:T(8,128)(2,1)} fusion(bf16[256,512]{0,1:T(8,128)(2,1)S(1)} %bitcast.60, bf16[512,8192]{1,0:T(8,128)(2,1)} %all-gather.9.cloned.1.call-done), kind=kOutput, calls=%fused_computation.21 | convolution fusion | flops 2149580800 | bytes 12845056 | tf_op jit(solution)/shard_map/dot_general | solution.py:87
  238.4 0.0 reduce-scatter.2.cloned.1.call-update
  238.5 242.1 %reduce-scatter.2.cloned.1.call-done = bf16[16,8192]{1,0:T(8,128)(2,1)} async-done(((bf16[256,8192]{1,0:T(8,128)(2,1)}), bf16[16,8192]{1,0:T(8,128)(2,1)}) %reduce-scatter.2.cloned.1.call-update) | async-done | bytes 262160 | tf_op jit(solution)/shard_map/reduce_scatter | solution.py:92
  (3 shorter events, 0.1 us)
Async XLA Ops:
  6.5 1.0 copy-start
  6.5 70.2 %all-gather.5.cloned.1.call-start = ((), (), s32[]{:S(2)}) async-start(), calls=%async_computation.1 | async-start | bytes 2162688 | tf_op jit(solution)/shard_map/all_gather | solution.py:73
  8.2 132.1 %all-gather.7.cloned.1.call-start = ((), (), s32[]{:S(2)}) async-start(), calls=%async_computation.2 | async-start | bytes 2162688 | tf_op jit(solution)/shard_map/all_gather | solution.py:74
  9.8 220.9 %all-gather.9.cloned.1.call-start = ((), (), s32[]{:S(2)}) async-start(), calls=%async_computation.3 | async-start | bytes 8650752 | tf_op jit(solution)/shard_map/all_gather | solution.py:89
  10.5 470.1 %reduce-scatter.2.cloned.1.call-start = ((), (), s32[]{:S(2)}) async-start(), calls=%async_computation.4 | async-start | bytes 4456448 | tf_op jit(solution)/shard_map/reduce_scatter | solution.py:92
Sparse Core Ops, SparseCore 0:
  9.5 67.2 all-gather.4
  78.9 61.4 all-gather.6
  142.4 88.2 all-gather.8
  238.6 241.9 reduce-scatter.1
where the time goes:
time: 488 us; the launch traced here: 487 us
  waiting for transfers between devices  368 us (75%)
  blocking collectives  43.7 us (9%)
  matrix products  38.2 us (8%)
  other arithmetic  19.2 us (4%)
  between operations  13.8 us (3%)
    reduce_scatter x1, waiting for transfers between devices, on_device(): lax.psum_scatter(terms.astype(jnp.bfloat16), 'tp', scatter_dimension=0, t...  242 us
    all_gather x1, waiting for transfers between devices, on_device(): lax.all_gather(own_values, 'ctx', axis=0, tiled=True)  63.6 us
    all_gather x1, blocking collectives, on_device(): lax.all_gather(documents, 'ctx', axis=0, tiled=True)  43.7 us
    all_gather x1, waiting for transfers between devices, on_device(): lax.all_gather(out_weight, 'ctx', axis=1, tiled=True)  40.4 us
    all_gather x1, waiting for transfers between devices, on_device(): lax.all_gather(own_keys, 'ctx', axis=0, tiled=True)  21.2 us
    dot_general x1, matrix products, update(): jnp.einsum('ghtn,ngd->tghd', weights.astype(jnp.bfloat16), value_block, p...  15.5 us
    dot_general x1, matrix products, update(): jnp.einsum('tghd,ngd->ghtn', query_block, key_block, preferred_element_ty...  14.9 us
    reduce_sum x1, other arithmetic, update(): new_sum = jnp.sum(weights, axis=3)  14.8 us
  transfers between devices with their start and end apart: 4, of which 4 were waited for; matrix products, arithmetic and copies ran while one was open for 11% of the time, Pallas kernels for 0%

commit v1 on v0

--- a/solution.py
+++ b/solution.py
@@ -71,7 +71,9 @@
     initial = tuple((empty_state(group[0].shape[0], kv_here, per_kv) for group in groups))
     piece = (
         lax.all_gather(own_keys, "ctx", axis=0, tiled=True),
-        lax.all_gather(own_values, "ctx", axis=0, tiled=True),
+        jnp.concatenate(
+            lax.all_to_all(jnp.stack([own_values] * lax.axis_size("ctx")), "ctx", 0, 0), axis=0
+        ),
         lax.all_gather(documents, "ctx", axis=0, tiled=True),
     )
     start = jnp.int32(0)

time: 488 us -> 438 us (0.90)
  waiting for transfers between devices: 368 us -> 273 us
  blocking collectives: 43.7 us -> 75.5 us
  starting transfers between devices: 0.12 us -> 10.5 us
    all_gather x1 -> x0, waiting for transfers between devices: 63.6 us -> none  [on_device(): lax.all_gather(own_values, 'ctx', axis=0, tiled=True)]
    all_gather x1, blocking collectives: 43.7 us -> 75.5 us  [on_device(): lax.all_gather(documents, 'ctx', axis=0, tiled=True)]
    all_gather x1, waiting for transfers between devices: 21.2 us -> 0.01 us  [on_device(): lax.all_gather(own_keys, 'ctx', axis=0, tiled=True)]
    all_gather x1, waiting for transfers between devices: 40.4 us -> 29.7 us  [on_device(): lax.all_gather(out_weight, 'ctx', axis=1, tiled=True)]
    all_to_all x0 -> x1, starting transfers between devices: none -> 10.4 us  [on_device(): lax.all_to_all(jnp.stack([own_values] * lax.axis_size('ctx')), 'ctx', 0, 0)]
  transfers between devices with their start and end apart: 4 -> 4, of which waited for: 4 -> 2; matrix products, arithmetic and copies ran while one was open for 11% -> 12% of each run, Pallas kernels for 0% -> 0%
where the time goes in v1:
time: 438 us
  waiting for transfers between devices  273 us (62%)
  blocking collectives  75.5 us (17%)
  matrix products  38.2 us (9%)
  other arithmetic  19.4 us (4%)
  between operations  13.8 us (3%)
  starting transfers between devices  10.5 us (2%)
  local copies, waits for them, and re-layouts  7.54 us (2%)
    reduce_scatter x1, waiting for transfers between devices, on_device(): lax.psum_scatter(terms.astype(jnp.bfloat16), 'tp', scatter_dimension=0, t...  242 us
    all_gather x1, blocking collectives, on_device(): lax.all_gather(documents, 'ctx', axis=0, tiled=True)  75.5 us
    all_gather x1, waiting for transfers between devices, on_device(): lax.all_gather(out_weight, 'ctx', axis=1, tiled=True)  29.7 us
    dot_general x1, matrix products, update(): jnp.einsum('ghtn,ngd->tghd', weights.astype(jnp.bfloat16), value_block, p...  15.4 us
    dot_general x1, matrix products, update(): jnp.einsum('tghd,ngd->ghtn', query_block, key_block, preferred_element_ty...  15 us
    reduce_sum x1, other arithmetic, update(): new_sum = jnp.sum(weights, axis=3)  14.9 us
    all_to_all x1, starting transfers between devices, on_device(): lax.all_to_all(jnp.stack([own_values] * lax.axis_size('ctx')), 'ctx', 0, 0)  10.4 us
  transfers between devices with their start and end apart: 4, of which 2 were waited for; matrix products, arithmetic and copies ran while one was open for 12% of the time, Pallas kernels for 0%

profile of v1, /device:TPU:2, one launch (start us, length us, event | category | flops | bytes accessed | tf_op | source)
XLA Modules:
  0.0 437.6 jit_solution(7548260403864477587)
XLA Ops:
  6.5 0.0 copy-start
  6.5 0.0 all-gather.4.cloned.1.call-start
  6.5 1.0 copy-done
  7.6 0.6 constant_dynamic-slice_fusion.1
  8.2 0.0 all-gather.4.cloned.1.call-update
  8.2 0.0 all-gather.6.cloned.1.call-start
  8.3 0.7 all-gather.6.cloned.1.call-update
  9.0 0.9 constant_dynamic-slice_fusion
  9.9 1.8 stack.2
  11.7 10.4 %all-to-all-start = ((bf16[32,256,128]{2,1,0:T(8,128)(2,1)}), bf16[32,256,128]{2,1,0:T(8,128)(2,1)S(1)}, u32[]{:S(2)}, u32[]{:S(2)}) async-start(bf16[32,256,128]{2,1,0:T(8,128)(2,1)} %stack.2), calls=%async_computation | async-start | bytes 4194304 | tf_op jit(solution)/shard_map/all_to_all | solution.py:75
  22.1 0.0 reduce-scatter.2.cloned.1.call-start
  22.2 0.6 slice.3
  23.5 75.5 %all-gather = s32[32,1,256]{2,1,0:T(1,128)S(1)} all-gather(s32[1,1,256]{2,1,0:T(1,128)} %bitcast.64), channel_id=1, replica_groups=mesh['ctx'=32,'tp'=16] {'ctx'}, dimensions={0}, use_global_device_ids=true | all-gather | bytes 33792 | tf_op jit(solution)/shard_map/all_gather | solution.py:77
  99.0 0.0 all-gather.4.cloned.1.call-done
  99.0 0.0 all-to-all-done
  99.0 52.4 %conditional.1 = (f32[1,4,256]{2,1,0:T(4,128)S(1)}, f32[256,1,4,128]{0,3,2,1:T(8,128)S(1)}) conditional(s32[]{:T(128)} %bitcast.11, () %tuple.13, (s32[256]{0:T(256)S(1)}, s32[8192]{0:T(1024)S(1)}, s32[256]{0:T(256)}, bf16[256,512]{1,0:T(8,128)(2,1)}, bf16[8192,128]{1,0:T(8,128)(2,1)}, /*index=5*/bf16[32,256,128]{2,1,0:T(8,128)(2,1)S(1)}) %tuple.26), branch_computations={%region_0.1_spmd, %region_1.4_spmd} | conditional | flops 4393532416 | bytes 131917896 | solution.py:41
  99.0 0.0 copy-start.1
  99.0 1.3 copy-done.1
  100.3 4.4 %fusion.9 = pred[256,8192]{0,1:T(8,128)(4,1)S(1)} fusion(s32[256]{0:T(256)} %get-tuple-element.20, s32[256]{0:T(256)S(1)} %get-tuple-element.18, s32[8192]{0:T(1024)S(1)} %get-tuple-element.19), kind=kLoop, calls=%fused_computation.11 | loop fusion | flops 6291456 | bytes 2131968 | tf_op jit(solution)/shard_map/cond/branch_1_fun/and | solution.py:27
  104.7 15.0 %fusion = (f32[4,256]{1,0:T(4,128)S(1)}, f32[8192,256,4]{1,0,2:T(8,128)}) fusion(pred[256,8192]{0,1:T(8,128)(4,1)S(1)} %fusion.9, bf16[8192,128]{1,0:T(8,128)(2,1)} %get-tuple-element.21, bf16[256,512]{1,0:T(8,128)(2,1)} %get-tuple-element.29), kind=kOutput, calls=%fused_computation.2 | convolution fusion | flops 2172648448 | bytes 38014976 | tf_op jit(solution)/shard_map/cond/branch_1_fun/tghd,ngd->ghtn/dot_general | solution.py:23
  119.8 0.0 copy-start.2
  119.8 14.9 %fusion.4 = f32[4,256]{1,0:T(4,128)S(1)} fusion(f32[8192,256,4]{1,0,2:T(8,128)} %get-tuple-element.32, f32[4,256]{1,0:T(4,128)S(1)} %broadcast_maximum_fusion, pred[256,8192]{0,1:T(8,128)(4,1)S(1)} %fusion.9), kind=kLoop, calls=%fused_computation.6 | loop fusion | flops 33553408 | bytes 35659776 | tf_op jit(solution)/shard_map/cond/branch_1_fun/reduce_sum | solution.py:32
  134.7 0.0 copy-done.2
  134.7 15.4 %fusion.12 = f32[256,1,4,128]{3,0,2,1:T(8,128)} fusion(bf16[8192,128,1]{1,0,2:T(8,128)(2,1)S(1)} %bitcast.59, f32[8192,256,4]{1,0,2:T(8,128)} %get-tuple-element.32, f32[4,256]{1,0:T(4,128)S(1)} %broadcast_maximum_fusion, pred[256,8192]{0,1:T(8,128)(4,1)S(1)} %fusion.9), kind=kOutput, calls=%fused_computation.14 | convolution fusion | flops 2181038080 | bytes 38277120 | tf_op jit(solution)/shard_map/cond/branch_1_fun/ghtn,ngd->tghd/dot_general | solution.py:33
  150.1 1.2 copy.17
  151.4 29.7 %all-gather.6.cloned.1.call-done = bf16[512,8192]{1,0:T(8,128)(2,1)} async-done(((bf16[512,256]{1,0:T(8,128)(2,1)}), bf16[512,8192]{1,0:T(8,128)(2,1)}) %all-gather.6.cloned.1.call-update) | async-done | bytes 8388624 | tf_op jit(solution)/shard_map/all_gather | solution.py:91
  181.1 7.7 %convolution_convert_fusion = bf16[256,8192]{1,0:T(8,128)(2,1)} fusion(bf16[256,512]{0,1:T(8,128)(2,1)S(1)} %bitcast.60, bf16[512,8192]{1,0:T(8,128)(2,1)} %all-gather.6.cloned.1.call-done), kind=kOutput, calls=%fused_computation.20 | convolution fusion | flops 2149580800 | bytes 12845056 | tf_op jit(solution)/shard_map/dot_general | solution.py:89
  188.8 0.0 reduce-scatter.2.cloned.1.call-update
  188.8 242.2 %reduce-scatter.2.cloned.1.call-done = bf16[16,8192]{1,0:T(8,128)(2,1)} async-done(((bf16[256,8192]{1,0:T(8,128)(2,1)}), bf16[16,8192]{1,0:T(8,128)(2,1)}) %reduce-scatter.2.cloned.1.call-update) | async-done | bytes 262160 | tf_op jit(solution)/shard_map/reduce_scatter | solution.py:94
  (3 shorter events, 0.1 us)
Async XLA Ops:
  6.5 1.0 copy-start
  6.5 92.5 %all-gather.4.cloned.1.call-start = ((), (), s32[]{:S(2)}) async-start(), calls=%async_computation.2 | async-start | bytes 2162688 | tf_op jit(solution)/shard_map/all_gather | solution.py:73
  8.2 172.9 %all-gather.6.cloned.1.call-start = ((), (), s32[]{:S(2)}) async-start(), calls=%async_computation.3 | async-start | bytes 8650752 | tf_op jit(solution)/shard_map/all_gather | solution.py:91
  11.7 87.3 %all-to-all-start = ((bf16[32,256,128]{2,1,0:T(8,128)(2,1)}), bf16[32,256,128]{2,1,0:T(8,128)(2,1)S(1)}, u32[]{:S(2)}, u32[]{:S(2)}) async-start(bf16[32,256,128]{2,1,0:T(8,128)(2,1)} %stack.2), calls=%async_computation | async-start | bytes 4194304 | tf_op jit(solution)/shard_map/all_to_all | solution.py:75
  22.1 408.9 %reduce-scatter.2.cloned.1.call-start = ((), (), s32[]{:S(2)}) async-start(), calls=%async_computation.4 | async-start | bytes 4456448 | tf_op jit(solution)/shard_map/reduce_scatter | solution.py:94
  99.0 1.3 copy-start.1
  119.8 14.9 %copy-start.2 = (bf16[32,256,128]{2,1,0:T(8,128)(2,1)S(1)}, bf16[32,256,128]{2,1,0:T(8,128)(2,1)}, u32[]{:S(2)}) copy-start(bf16[32,256,128]{2,1,0:T(8,128)(2,1)} %copy-done.1) | copy-start | bytes 6291460 | tf_op jit(solution)/shard_map/cond
Sparse Core Ops, SparseCore 0:
  9.5 78.1 all-gather.3
  89.8 91.2 all-gather.5
  188.9 242.0 reduce-scatter.1
